TPU v7x, 32 devices: a whole 2x2x4 slice. The times are simulated.
32 devices in a mesh: replica: 8 (over z, y), shard: 4 (over x, core).
Axes of the slice: x: 2, y: 2, z: 4, core: 2. Of those that a mesh axis runs over, the one named last changes fastest.
Arguments:
- hidden_in: bfloat16 [4096, 1024], P(('replica', 'shard')), may hold values from -6 to 6
- out_grad: bfloat16 [4096, 1024], P(('replica', 'shard')), may hold values from -6 to 6
- lengths: int32 [32, 4], P(('replica', 'shard')), may hold values from 1 to 64, 128 in all within a row
- norm1_gain: bfloat16 [1024], P('shard'), may hold values from 0.099609375 to 1.8984375
- norm1_bias: bfloat16 [1024], P('shard'), may hold values from -3 to 3
- qkv_weight: bfloat16 [1024, 3072], P('shard'), may hold values from -0.1875 to 0.1875
- query_bias: bfloat16 [1024], P('shard'), may hold values from -3 to 3
- value_bias: bfloat16 [1024], P('shard'), may hold values from -3 to 3
- out_weight: bfloat16 [1024, 1024], P('shard'), may hold values from -0.75 to 0.75
- out_bias: bfloat16 [1024], P('shard'), may hold values from -3 to 3
- norm2_gain: bfloat16 [1024], P('shard'), may hold values from 0.099609375 to 1.8984375
- norm2_bias: bfloat16 [1024], P('shard'), may hold values from -3 to 3
- up_weight: bfloat16 [1024, 4096], P('shard'), may hold values from -0.1875 to 0.1875
- up_bias: bfloat16 [4096], P('shard'), may hold values from -3 to 3
- down_weight: bfloat16 [4096, 1024], P('shard'), may hold values from -0.125 to 0.125
- down_bias: bfloat16 [1024], P('shard'), may hold values from -3 to 3
Outputs:
- hidden_out: bfloat16 [4096, 1024], P(('replica', 'shard'))
- in_grad: bfloat16 [4096, 1024], P(('replica', 'shard'))
- norm1_gain_grad: float32 [1024], P('shard')
- norm1_bias_grad: float32 [1024], P('shard')
- qkv_weight_grad: float32 [1024, 3072], P('shard')
- query_bias_grad: float32 [1024], P('shard')
- value_bias_grad: float32 [1024], P('shard')
- out_weight_grad: float32 [1024, 1024], P('shard')
- out_bias_grad: float32 [1024], P('shard')
- norm2_gain_grad: float32 [1024], P('shard')
- norm2_bias_grad: float32 [1024], P('shard')
- up_weight_grad: float32 [1024, 4096], P('shard')
- up_bias_grad: float32 [4096], P('shard')
- down_weight_grad: float32 [4096, 1024], P('shard')
- down_bias_grad: float32 [1024], P('shard')
Inputs may be any that keep to these rules, and one draw needn't show every extreme that they name: The 4 lengths of each device add up to 128, and the largest of all is 64.
All inputs are finite; a program needn't handle non-finite values.
Results may differ from a plain program's by a relative error of at most 0.018.
Values may be sent and summed in bfloat16 or wider, within the bound.
A program may use at most 192 MiB of HBM per device.

v0:
```python
import math
import jax
import jax.numpy as jnp
from jax import lax
from jax.sharding import PartitionSpec as P

HEADS = 16
HEAD_DIM = 64
EPSILON = 1e-05
TANH_SCALE = math.sqrt(2.0 / math.pi)
CUBIC = 0.044715


def product(left, right):
    return jnp.dot(left, right, preferred_element_type=jnp.float32)


def left_product(left, right):
    return lax.dot_general(
        left, right, (((0,), (0,)), ((), ())), preferred_element_type=jnp.float32
    )


def right_product(left, right):
    return lax.dot_general(
        left, right, (((1,), (1,)), ((), ())), preferred_element_type=jnp.float32
    )


def column_term(left, right):
    return left_product(left, right)


def gelu_parts(pre_act):
    inner_arg = TANH_SCALE * (pre_act + CUBIC * pre_act * pre_act * pre_act)
    tangent = jnp.tanh(inner_arg)
    gelu_value = 0.5 * pre_act * (1.0 + tangent)
    gelu_slope = 0.5 * (1.0 + tangent) + 0.5 * pre_act * (1.0 - tangent * tangent) * TANH_SCALE * (
        1.0 + 3.0 * CUBIC * pre_act * pre_act
    )
    return (gelu_value, gelu_slope)


def layer_norm(inputs, gain_row, bias_row):
    average = jnp.mean(inputs, axis=-1, keepdims=True)
    centred = inputs - average
    inv_std = lax.rsqrt(jnp.mean(centred * centred, axis=-1, keepdims=True) + EPSILON)
    normed = centred * inv_std
    return (normed * gain_row.astype(jnp.float32) + bias_row.astype(jnp.float32), normed, inv_std)


def norm_back(upstream, normed, inv_std, gain_row):
    scaled = upstream * gain_row.astype(jnp.float32)
    first_term = jnp.mean(scaled, axis=-1, keepdims=True)
    second_term = jnp.mean(scaled * normed, axis=-1, keepdims=True)
    input_grad = inv_std * (scaled - first_term - normed * second_term)
    return (input_grad, jnp.sum(upstream * normed, axis=0), jnp.sum(upstream, axis=0))


def seq_mask(lengths, row_count):
    seq_ends = jnp.cumsum(lengths, axis=-1)
    places = jnp.arange(row_count, dtype=jnp.int32)
    segment = jnp.sum((places[None, :, None] >= seq_ends[:, None, :]).astype(jnp.int32), axis=-1)
    causal = places[None, :] <= places[:, None]
    return (segment[:, :, None] == segment[:, None, :]) & causal[None]


def split_heads(flat_rows, groups):
    return flat_rows.reshape(groups, -1, HEADS, HEAD_DIM)


def attend_forward(queries, key_rows, values, allowed):
    groups = allowed.shape[0]
    scale_factor = 1.0 / math.sqrt(HEAD_DIM)
    head_q = split_heads(queries, groups)
    head_k = split_heads(key_rows, groups)
    head_v = split_heads(values, groups)
    scores = (
        jnp.einsum("gqhd,gkhd->ghqk", head_q, head_k, preferred_element_type=jnp.float32)
        * scale_factor
    )
    visible = allowed[:, None]
    row_total = jnp.sum(jnp.where(visible, jnp.exp(scores), 0.0), axis=-1, keepdims=True)
    log_total = jnp.log(row_total)
    probs_round = jnp.where(visible, jnp.exp(scores - log_total), 0.0).astype(jnp.bfloat16)
    context = jnp.einsum("ghqk,gkhd->gqhd", probs_round, head_v, preferred_element_type=jnp.float32)
    return (context.reshape(-1, HEADS * HEAD_DIM).astype(jnp.bfloat16), log_total)


def attend_backward(queries, key_rows, values, allowed, log_total, context_grad):
    groups = allowed.shape[0]
    scale_factor = 1.0 / math.sqrt(HEAD_DIM)
    head_q = split_heads(queries, groups)
    head_k = split_heads(key_rows, groups)
    head_v = split_heads(values, groups)
    head_g = split_heads(context_grad, groups)
    scores = (
        jnp.einsum("gqhd,gkhd->ghqk", head_q, head_k, preferred_element_type=jnp.float32)
        * scale_factor
    )
    visible = allowed[:, None]
    exact_probs = jnp.where(visible, jnp.exp(scores - log_total), 0.0)
    probs_round = exact_probs.astype(jnp.bfloat16)
    prob_grad = jnp.einsum("gqhd,gkhd->ghqk", head_g, head_v, preferred_element_type=jnp.float32)
    value_grad = jnp.einsum(
        "ghqk,gqhd->gkhd", probs_round, head_g, preferred_element_type=jnp.float32
    )
    row_delta = jnp.sum(exact_probs * prob_grad, axis=-1, keepdims=True)
    score_grad = (exact_probs * (prob_grad - row_delta) * scale_factor).astype(jnp.bfloat16)
    query_grad = jnp.einsum(
        "ghqk,gkhd->gqhd", score_grad, head_k, preferred_element_type=jnp.float32
    )
    key_grad = jnp.einsum("ghqk,gqhd->gkhd", score_grad, head_q, preferred_element_type=jnp.float32)
    model_width = HEADS * HEAD_DIM
    return (
        query_grad.reshape(-1, model_width),
        key_grad.reshape(-1, model_width),
        value_grad.reshape(-1, model_width),
    )


def local(
    hidden_in,
    out_grad,
    lengths,
    norm1_gain,
    norm1_bias,
    qkv_weight,
    query_bias,
    value_bias,
    out_weight,
    out_bias,
    norm2_gain,
    norm2_bias,
    up_weight,
    up_bias,
    down_weight,
    down_bias,
):
    (
        gain_one,
        bias_one,
        qkv_full,
        qbias_full,
        vbias_full,
        outw_full,
        outb_full,
        gain_two,
        bias_two,
        upw_full,
        upb_full,
        downw_full,
        downb_full,
    ) = (
        lax.all_gather(norm1_gain, "shard", axis=0, tiled=True),
        lax.all_gather(norm1_bias, "shard", axis=0, tiled=True),
        lax.all_gather(qkv_weight, "shard", axis=0, tiled=True),
        lax.all_gather(query_bias, "shard", axis=0, tiled=True),
        lax.all_gather(value_bias, "shard", axis=0, tiled=True),
        lax.all_gather(out_weight, "shard", axis=0, tiled=True),
        lax.all_gather(out_bias, "shard", axis=0, tiled=True),
        lax.all_gather(norm2_gain, "shard", axis=0, tiled=True),
        lax.all_gather(norm2_bias, "shard", axis=0, tiled=True),
        lax.all_gather(up_weight, "shard", axis=0, tiled=True),
        lax.all_gather(up_bias, "shard", axis=0, tiled=True),
        lax.all_gather(down_weight, "shard", axis=0, tiled=True),
        lax.all_gather(down_bias, "shard", axis=0, tiled=True),
    )
    allowed = seq_mask(lengths, hidden_in.shape[0])
    model_width = hidden_in.shape[1]
    inputs_wide = hidden_in.astype(jnp.float32)
    first_out, normed_one, inv_one = layer_norm(inputs_wide, gain_one, bias_one)
    first_in = first_out.astype(jnp.bfloat16)
    projected = product(first_in, qkv_full)
    queries = (projected[:, :model_width] + qbias_full.astype(jnp.float32)).astype(jnp.bfloat16)
    key_rows = projected[:, model_width : 2 * model_width].astype(jnp.bfloat16)
    values = (projected[:, 2 * model_width :] + vbias_full.astype(jnp.float32)).astype(jnp.bfloat16)
    context, log_total = attend_forward(queries, key_rows, values, allowed)
    residual = inputs_wide + product(context, outw_full) + outb_full.astype(jnp.float32)
    second_out, normed_two, inv_two = layer_norm(residual, gain_two, bias_two)
    second_in = second_out.astype(jnp.bfloat16)
    pre_act = product(second_in, upw_full) + upb_full.astype(jnp.float32)
    activ_value, gelu_slope = gelu_parts(pre_act)
    activated = activ_value.astype(jnp.bfloat16)
    hidden_out = (
        residual + product(activated, downw_full) + downb_full.astype(jnp.float32)
    ).astype(jnp.bfloat16)
    back_qkv, back_out, back_up, back_down, back_gain1, back_gain2 = (
        qkv_full,
        outw_full,
        upw_full,
        downw_full,
        gain_one,
        gain_two,
    )
    upstream = out_grad.astype(jnp.float32)
    down_owned = lax.psum_scatter(
        column_term(activated, out_grad).astype(jnp.bfloat16),
        "shard",
        scatter_dimension=0,
        tiled=True,
    )
    down_bgrad = jnp.sum(upstream, axis=0)
    pre_grad = right_product(out_grad, back_down) * gelu_slope
    pre_round = pre_grad.astype(jnp.bfloat16)
    up_bgrad = jnp.sum(pre_grad, axis=0)
    up_owned = lax.psum_scatter(
        column_term(second_in, pre_round).astype(jnp.bfloat16),
        "shard",
        scatter_dimension=0,
        tiled=True,
    )
    second_grad = right_product(pre_round, back_up)
    norm_two_in, gain2_grad, bias2_grad = norm_back(second_grad, normed_two, inv_two, back_gain2)
    resid_grad = upstream + norm_two_in
    resid_round = resid_grad.astype(jnp.bfloat16)
    out_bgrad = jnp.sum(resid_grad, axis=0)
    out_owned = lax.psum_scatter(
        column_term(context, resid_round).astype(jnp.bfloat16),
        "shard",
        scatter_dimension=0,
        tiled=True,
    )
    context_grad = right_product(resid_round, back_out).astype(jnp.bfloat16)
    query_grad, key_grad, value_grad = attend_backward(
        queries, key_rows, values, allowed, log_total, context_grad
    )
    query_bgrad = jnp.sum(query_grad, axis=0)
    value_bgrad = jnp.sum(value_grad, axis=0)
    qkv_grad = jnp.concatenate([query_grad, key_grad, value_grad], axis=1).astype(jnp.bfloat16)
    qkv_owned = lax.psum_scatter(
        column_term(first_in, qkv_grad).astype(jnp.bfloat16),
        "shard",
        scatter_dimension=0,
        tiled=True,
    )
    first_grad = right_product(qkv_grad, back_qkv)
    norm_one_in, gain1_grad, bias1_grad = norm_back(first_grad, normed_one, inv_one, back_gain1)
    in_grad = (resid_grad + norm_one_in).astype(jnp.bfloat16)
    (
        gain1_own,
        bias1_own,
        qbias_own,
        vbias_own,
        outb_own,
        gain2_own,
        bias2_own,
        upb_own,
        downb_own,
    ) = (
        lax.psum_scatter(
            gain1_grad.astype(jnp.bfloat16), "shard", scatter_dimension=0, tiled=True
        ).astype(jnp.float32),
        lax.psum_scatter(
            bias1_grad.astype(jnp.bfloat16), "shard", scatter_dimension=0, tiled=True
        ).astype(jnp.float32),
        lax.psum_scatter(
            query_bgrad.astype(jnp.bfloat16), "shard", scatter_dimension=0, tiled=True
        ).astype(jnp.float32),
        lax.psum_scatter(
            value_bgrad.astype(jnp.bfloat16), "shard", scatter_dimension=0, tiled=True
        ).astype(jnp.float32),
        lax.psum_scatter(
            out_bgrad.astype(jnp.bfloat16), "shard", scatter_dimension=0, tiled=True
        ).astype(jnp.float32),
        lax.psum_scatter(
            gain2_grad.astype(jnp.bfloat16), "shard", scatter_dimension=0, tiled=True
        ).astype(jnp.float32),
        lax.psum_scatter(
            bias2_grad.astype(jnp.bfloat16), "shard", scatter_dimension=0, tiled=True
        ).astype(jnp.float32),
        lax.psum_scatter(
            up_bgrad.astype(jnp.bfloat16), "shard", scatter_dimension=0, tiled=True
        ).astype(jnp.float32),
        lax.psum_scatter(
            down_bgrad.astype(jnp.bfloat16), "shard", scatter_dimension=0, tiled=True
        ).astype(jnp.float32),
    )
    (
        gain1_total,
        bias1_total,
        qkv_total,
        qbias_total,
        vbias_total,
        outw_total,
        outb_total,
        gain2_total,
        bias2_total,
        upw_total,
        upb_total,
        downw_total,
        downb_total,
    ) = (
        lax.psum(gain1_own.astype(jnp.bfloat16), "replica").astype(jnp.float32),
        lax.psum(bias1_own.astype(jnp.bfloat16), "replica").astype(jnp.float32),
        lax.psum(qkv_owned, "replica").astype(jnp.float32),
        lax.psum(qbias_own.astype(jnp.bfloat16), "replica").astype(jnp.float32),
        lax.psum(vbias_own.astype(jnp.bfloat16), "replica").astype(jnp.float32),
        lax.psum(out_owned, "replica").astype(jnp.float32),
        lax.psum(outb_own.astype(jnp.bfloat16), "replica").astype(jnp.float32),
        lax.psum(gain2_own.astype(jnp.bfloat16), "replica").astype(jnp.float32),
        lax.psum(bias2_own.astype(jnp.bfloat16), "replica").astype(jnp.float32),
        lax.psum(up_owned, "replica").astype(jnp.float32),
        lax.psum(upb_own.astype(jnp.bfloat16), "replica").astype(jnp.float32),
        lax.psum(down_owned, "replica").astype(jnp.float32),
        lax.psum(downb_own.astype(jnp.bfloat16), "replica").astype(jnp.float32),
    )
    return (
        hidden_out,
        in_grad,
        gain1_total,
        bias1_total,
        qkv_total,
        qbias_total,
        vbias_total,
        outw_total,
        outb_total,
        gain2_total,
        bias2_total,
        upw_total,
        upb_total,
        downw_total,
        downb_total,
    )


def solution(mesh):
    in_specs = (
        P(("replica", "shard"), None),
        P(("replica", "shard"), None),
        P(("replica", "shard"), None),
        P("shard"),
        P("shard"),
        P("shard", None),
        P("shard"),
        P("shard"),
        P("shard", None),
        P("shard"),
        P("shard"),
        P("shard"),
        P("shard", None),
        P("shard"),
        P("shard", None),
        P("shard"),
    )
    out_specs = (
        P(("replica", "shard"), None),
        P(("replica", "shard"), None),
        P("shard"),
        P("shard"),
        P("shard", None),
        P("shard"),
        P("shard"),
        P("shard", None),
        P("shard"),
        P("shard"),
        P("shard"),
        P("shard", None),
        P("shard"),
        P("shard", None),
        P("shard"),
    )
    return jax.shard_map(local, mesh=mesh, in_specs=in_specs, out_specs=out_specs, check_vma=False)
```

profile of v0, /device:TPU:0, one launch (start us, length us, event | category | flops | bytes accessed | tf_op | source)
XLA Modules:
  0.0 687.5 jit_solution(8565300499013674690)
XLA Ops:
  7.2 0.7 all-gather.13.cloned.1.call-update
  8.0 0.7 all-gather.15.cloned.1.call-update
  8.8 0.7 all-gather.17.cloned.1.call-update
  9.5 0.5 all-gather.19.cloned.1.call-update
  10.1 6.0 all-gather.4
  16.2 5.4 all-gather.1
  21.6 5.2 all-gather
  26.8 5.2 all-gather.3
  32.0 5.2 all-gather.2
  37.3 5.4 all_gather.49
  42.6 5.2 all-gather.6
  47.9 5.2 all-gather.5
  53.5 0.2 fusion.38
  53.8 5.0 all-gather.13.cloned.1.call-done
  58.8 3.9 fusion.66
  63.4 0.4 convolution_multiply_fusion.1
  63.8 0.5 convolution_convert_fusion.6
  64.3 18.7 %all-gather.15.cloned.1.call-done = bf16[1024,1024]{1,0:T(8,128)(2,1)} async-done(((bf16[256,1024]{1,0:T(8,128)(2,1)}), bf16[1024,1024]{1,0:T(8,128)(2,1)}) %all-gather.15.cloned.1.call-update) | async-done | bytes 2097168 | tf_op jit(solution)/shard_map/all_gather | solution.py:160
  83.0 2.1 fusion.71
  85.1 0.2 multiply_reduce_fusion.3
  85.4 57.5 %all-gather.17.cloned.1.call-done = bf16[1024,4096]{1,0:T(8,128)(2,1)} async-done(((bf16[256,4096]{1,0:T(8,128)(2,1)}), bf16[1024,4096]{1,0:T(8,128)(2,1)}) %all-gather.17.cloned.1.call-update) | async-done | bytes 8388624 | tf_op jit(solution)/shard_map/all_gather | solution.py:164
  142.8 4.8 convolution_add_fusion
  147.6 54.9 %all-gather.19.cloned.1.call-done = bf16[4096,1024]{1,0:T(8,128)(2,1)} async-done(((bf16[1024,1024]{1,0:T(8,128)(2,1)}), bf16[4096,1024]{1,0:T(8,128)(2,1)}) %all-gather.19.cloned.1.call-update) | async-done | bytes 8388624 | tf_op jit(solution)/shard_map/all_gather | solution.py:166
  202.5 7.1 %fusion.74 = (bf16[4096]{0:T(1024)(128)(2,1)S(1)}, bf16[128,4096]{1,0:T(8,128)(2,1)S(1)}) fusion(f32[128,4096]{1,0:T(8,128)S(1)} %convolution_add_fusion, bf16[128,1024]{1,0:T(8,128)(2,1)S(1)} %copy-done.4, bf16[4096,1024]{1,0:T(8,128)(2,1)} %all-gather.19.cloned.1.call-done), kind=kOutput, calls=%fused_computation.108 | convolution fusion | flops 1084223488 | bytes 11804672 | tf_op jit(solution)/shard_map/dot_general | solution.py:25
  209.6 3.0 multiply_reduce_fusion.1
  212.7 0.3 fusion.68
  213.0 2.0 convolution_convert_fusion.3
  215.0 0.2 reduce-scatter.5.cloned.1.call-start
  215.3 3.0 fusion.13
  218.2 1.5 convolution_convert_fusion.5
  219.8 1.9 copy.63
  221.7 3.2 fusion.69
  224.8 2.4 fusion.75
  227.2 3.6 convolution_convert_fusion.4
  230.8 3.7 fusion.70
  234.5 5.8 convolution_convert_fusion.2
  240.4 6.9 %convolution_convert_fusion.1 = bf16[1024,4096]{1,0:T(8,128)(2,1)} fusion(bf16[128,4096]{1,0:T(8,128)(2,1)} %copy-done.3, f32[128,1024]{1,0:T(8,128)S(1)} %get-tuple-element.54, f32[1024]{0:T(1024)S(1)} %bitcast.77, f32[1024]{0:T(1024)S(1)} %bitcast.69, f32[128]{0:T(128)S(1)} %add_rsqrt_fusion, f32[128]{0:T(128)S(1)} %broadcast_multiply_fusion.4), kind=kOutput, calls=%fused_computation.3 | convolution fusion | flops 1078591488 | bytes 9970688 | tf_op jit(solution)/shard_map/dot_general | solution.py:19
  247.3 6.6 convolution_convert_fusion
  254.0 53.6 %reduce-scatter.5.cloned.1.call-done = bf16[256,3072]{1,0:T(8,128)(2,1)} async-done(((bf16[1024,3072]{1,0:T(8,128)(2,1)}), bf16[256,3072]{1,0:T(8,128)(2,1)}) %reduce-scatter.5.cloned.1.call-update) | async-done | bytes 1572880 | tf_op jit(solution)/shard_map/reduce_scatter | solution.py:231
  307.6 74.0 %reduce-scatter.9.cloned.1.call-done = bf16[256,4096]{1,0:T(8,128)(2,1)} async-done(((bf16[1024,4096]{1,0:T(8,128)(2,1)}), bf16[256,4096]{1,0:T(8,128)(2,1)}) %reduce-scatter.9.cloned.1.call-update) | async-done | bytes 2097168 | tf_op jit(solution)/shard_map/reduce_scatter | solution.py:207
  381.6 74.0 %reduce-scatter.11.cloned.1.call-done = bf16[1024,1024]{1,0:T(8,128)(2,1)} async-done(((bf16[4096,1024]{1,0:T(8,128)(2,1)}), bf16[1024,1024]{1,0:T(8,128)(2,1)}) %reduce-scatter.11.cloned.1.call-update) | async-done | bytes 2097168 | tf_op jit(solution)/shard_map/reduce_scatter | solution.py:197
  455.7 0.6 copy-done.24
  456.3 5.1 all-gather.7
  461.4 1.0 reduce_sum.202
  462.4 0.6 dynamic-slice
  464.4 6.9 fusion.37
  471.3 11.3 %all-reduce.11 = (bf16[1024]{0:T(1024)(128)(2,1)S(1)}, bf16[1024]{0:T(1024)(128)(2,1)S(1)}, bf16[1024]{0:T(1024)(128)(2,1)S(1)}, bf16[1024]{0:T(1024)(128)(2,1)S...) all-reduce(bf16[1024]{0:T(1024)(128)(2,1)S(1)} %get-tuple-element.1, ...), channel_id=2, replica_groups=mesh['replica'=8,'shard'=4] {'shard'}, use_global_device_ids=true, to_apply=%region_13.14.clone | all-reduce | flops 12288 | bytes 49152
  483.2 23.3 %all-reduce.9 = (bf16[256]{0:T(256)(128)(2,1)S(1)}, bf16[256]{0:T(256)(128)(2,1)S(1)}, bf16[256]{0:T(256)(128)(2,1)S(1)}, bf16[256]{0:T(256)(128)(2,1)S(1)}, bf1...) all-reduce(bf16[256]{0:T(256)(128)(2,1)S(1)} %dynamic-slice.1, ...), channel_id=1, replica_groups=mesh['replica'=8,'shard'=4] {'replica'}, use_global_device_ids=true, to_apply=%region_14.15 | all-reduce | flops 3072 | bytes 12288 | tf_op jit(solution)/shard_map/psum | solution.py:294
  506.4 0.6 convert_element_type.228
  507.0 0.6 convert_element_type.230
  507.6 0.6 convert_element_type.235
  508.1 0.6 convert_element_type.238
  508.7 0.6 convert_element_type.242
  509.3 0.6 convert_element_type.244
  509.8 0.6 convert_element_type.246
  510.4 0.6 convert_element_type.250
  511.0 0.6 convert_element_type.253
  511.6 2.0 fusion.36
  513.6 5.6 fusion.17
  519.2 152.1 %all-reduce.14.cloned.1.call-done = (bf16[256,3072]{1,0:T(8,128)(2,1)}, bf16[256,1024]{1,0:T(8,128)(2,1)}, bf16[256,4096]{1,0:T(8,128)(2,1)}, bf16[1024,1024]{1,0:T(8,128)(2,1)}) async-done(((bf16[256,3072]{1,0:T(8,128)(2,1)}, bf16[256,1024]{1,0:T(8,128)(2,1)}, bf16[256,4096]{1,0:T(8,128)(2,1)}, bf16[1024,1024]{1,0:T(8,128)(2,1)}), (bf16[256,3072]{1,0:T(8,128)(2,1)}, bf16[256,1024]{1,0:T(8,128)(2,1)}, ...) | async-done | bytes 6291472 | tf_op jit(solution)/shard_map/psum | solution.py:296
  671.3 3.6 convert_element_type.232
  674.9 1.1 convert_element_type.240
  676.0 2.5 convert_element_type.248
  678.5 2.5 convert_element_type.252
  (109 shorter events, 2.5 us)
Async XLA Ops:
  7.2 51.6 %all-gather.13.cloned.1.call-start = ((), (), s32[]{:S(2)}) async-start(), calls=%async_computation.4 | async-start | bytes 7864320 | tf_op jit(solution)/shard_map/all_gather | solution.py:157
  7.9 75.1 %all-gather.15.cloned.1.call-start = ((), (), s32[]{:S(2)}) async-start(), calls=%async_computation.5 | async-start | bytes 2621440 | tf_op jit(solution)/shard_map/all_gather | solution.py:160
  8.7 1.5 copy-start.16
  8.7 7.5 %copy-start.17 = (bf16[256]{0:T(256)(128)(2,1)S(1)}, bf16[256]{0:T(256)(128)(2,1)}, u32[]{:S(2)}) copy-start(bf16[256]{0:T(256)(128)(2,1)} %param.20) | copy-start | bytes 1540
  8.7 12.9 %copy-start.18 = (bf16[256]{0:T(256)(128)(2,1)S(1)}, bf16[256]{0:T(256)(128)(2,1)}, u32[]{:S(2)}) copy-start(bf16[256]{0:T(256)(128)(2,1)} %param.19) | copy-start | bytes 1540
  8.7 18.1 %copy-start.19 = (bf16[256]{0:T(256)(128)(2,1)S(1)}, bf16[256]{0:T(256)(128)(2,1)}, u32[]{:S(2)}) copy-start(bf16[256]{0:T(256)(128)(2,1)} %param.22) | copy-start | bytes 1540
  8.7 23.3 %copy-start.20 = (bf16[256]{0:T(256)(128)(2,1)S(1)}, bf16[256]{0:T(256)(128)(2,1)}, u32[]{:S(2)}) copy-start(bf16[256]{0:T(256)(128)(2,1)} %param.23) | copy-start | bytes 1540
  8.7 28.5 %copy-start.15 = (bf16[1024]{0:T(1024)(128)(2,1)S(1)}, bf16[1024]{0:T(1024)(128)(2,1)}, u32[]{:S(2)}) copy-start(bf16[1024]{0:T(1024)(128)(2,1)} %param.29) | copy-start | bytes 6148
  8.7 33.9 %copy-start.21 = (bf16[256]{0:T(256)(128)(2,1)S(1)}, bf16[256]{0:T(256)(128)(2,1)}, u32[]{:S(2)}) copy-start(bf16[256]{0:T(256)(128)(2,1)} %param.27) | copy-start | bytes 1540
  8.7 39.1 %copy-start.22 = (bf16[256]{0:T(256)(128)(2,1)S(1)}, bf16[256]{0:T(256)(128)(2,1)}, u32[]{:S(2)}) copy-start(bf16[256]{0:T(256)(128)(2,1)} %param.26) | copy-start | bytes 1540
  8.7 44.3 %copy-start.23 = (s32[1,4]{1,0:T(1,128)S(1)}, s32[1,4]{1,0:T(1,128)}, u32[]{:S(2)}) copy-start(s32[1,4]{1,0:T(1,128)} %param.18) | copy-start | bytes 52
  8.8 44.6 %copy-start.1 = (bf16[128,1024]{1,0:T(8,128)(2,1)S(1)}, bf16[128,1024]{1,0:T(8,128)(2,1)}, u32[]{:S(2)}) copy-start(bf16[128,1024]{1,0:T(8,128)(2,1)} %param.16) | copy-start | bytes 786436
  8.8 134.1 %all-gather.17.cloned.1.call-start = ((), (), s32[]{:S(2)}) async-start(), calls=%async_computation.6 | async-start | bytes 10485760 | tf_op jit(solution)/shard_map/all_gather | solution.py:164
  9.5 193.0 %all-gather.19.cloned.1.call-start = ((), (), s32[]{:S(2)}) async-start(), calls=%async_computation.7 | async-start | bytes 10485760 | tf_op jit(solution)/shard_map/all_gather | solution.py:166
  10.1 243.9 %reduce-scatter.7.cloned.1.call-start = ((), (), s32[]{:S(2)}) async-start(), calls=%async_computation.9 | async-start | bytes 2621440 | tf_op jit(solution)/shard_map/reduce_scatter | solution.py:218
  63.0 1.2 copy-start.10
  63.2 21.9 %copy-start.11 = (bf16[128,1024]{0,1:T(8,128)(2,1)}, bf16[128,1024]{0,1:T(8,128)(2,1)S(1)}, u32[]{:S(2)}) copy-start(bf16[128,1024]{0,1:T(8,128)(2,1)S(1)} %copy.60) | copy-start | bytes 786436
  63.4 21.7 %copy-start.9 = (bf16[128,1024]{0,1:T(8,128)(2,1)}, bf16[128,1024]{0,1:T(8,128)(2,1)S(1)}, u32[]{:S(2)}) copy-start(bf16[128,1024]{0,1:T(8,128)(2,1)S(1)} %copy.61) | copy-start | bytes 786436
  63.8 19.2 %copy-start.8 = (f32[16,128,128]{1,2,0:T(8,128)}, f32[16,128,128]{1,2,0:T(8,128)S(1)}, u32[]{:S(2)}) copy-start(f32[16,128,128]{1,2,0:T(8,128)S(1)} %convolution_multiply_fusion.1) | copy-start | bytes 3145732
  64.3 78.6 %copy-start.12 = (bf16[16,64,128]{2,1,0:T(8,128)(2,1)}, bf16[16,64,128]{2,1,0:T(8,128)(2,1)S(1)}, u32[]{:S(2)}) copy-start(bf16[16,64,128]{2,1,0:T(8,128)(2,1)S(1)} %convolution_convert_fusion.6) | copy-start | bytes 786436
  142.8 59.7 %copy-start.4 = (bf16[128,1024]{1,0:T(8,128)(2,1)S(1)}, bf16[128,1024]{1,0:T(8,128)(2,1)}, u32[]{:S(2)}) copy-start(bf16[128,1024]{1,0:T(8,128)(2,1)} %param.17) | copy-start | bytes 786436
  202.5 7.1 %copy-start = (bf16[1024,4096]{1,0:T(8,128)(2,1)S(1)}, bf16[1024,4096]{1,0:T(8,128)(2,1)}, u32[]{:S(2)}) copy-start(bf16[1024,4096]{1,0:T(8,128)(2,1)} %all-gather.17.cloned.1.call-done) | copy-start | bytes 25165828
  209.6 3.1 copy-start.3
  209.6 3.1 copy-start.5
  209.6 3.3 copy-start.13
  215.0 92.6 %reduce-scatter.5.cloned.1.call-start = ((), (), s32[]{:S(2)}) async-start(), calls=%async_computation.8 | async-start | bytes 7864320 | tf_op jit(solution)/shard_map/reduce_scatter | solution.py:231
  215.2 3.0 copy-start.2
  240.3 141.3 %reduce-scatter.9.cloned.1.call-start = ((), (), s32[]{:S(2)}) async-start(), calls=%async_computation.10 | async-start | bytes 10485760 | tf_op jit(solution)/shard_map/reduce_scatter | solution.py:207
  247.3 208.4 %reduce-scatter.11.cloned.1.call-start = ((), (), s32[]{:S(2)}) async-start(), calls=%async_computation.11 | async-start | bytes 10485760 | tf_op jit(solution)/shard_map/reduce_scatter | solution.py:197
  253.9 417.3 %all-reduce.14.cloned.1.call-start = ((), (), s32[]{:S(2)}) async-start(), calls=%async_computation.12 | async-start | bytes 12582912 | tf_op jit(solution)/shard_map/psum | solution.py:296
  455.7 0.7 copy-start.24
  455.7 6.7 copy-start.25
  671.3 3.6 copy-start.14
  671.3 4.7 copy-start.7
  676.0 2.5 copy-start.6
Sparse Core Ops, SparseCore 0:
  9.6 49.2 all-gather.12
  60.4 22.5 all-gather.14
  84.5 58.2 all-gather.16
  144.2 58.2 all-gather.18
  215.1 31.1 reduce-scatter.6
  248.7 58.8 reduce-scatter.4
  310.2 71.3 reduce-scatter.8
  384.2 71.4 reduce-scatter.10
  460.1 211.1 all-reduce.13
where the time goes:
time: 688 us; the launch traced here: 687 us
  waiting for transfers between devices  493 us (72%)
  blocking collectives  82.4 us (12%)
  matrix products  69.8 us (10%)
  other arithmetic  22.1 us (3%)
  between operations  15.6 us (2%)
    psum x1, waiting for transfers between devices, local(): lax.psum(qkv_owned, 'replica').astype(jnp.float32)  152 us
    reduce_scatter x1, waiting for transfers between devices, local(): lax.psum_scatter(column_term(activated, out_grad).astype(jnp.bfloat16), '...  74 us
    reduce_scatter x1, waiting for transfers between devices, local(): lax.psum_scatter(column_term(second_in, pre_round).astype(jnp.bfloat16),...  74 us
    all_gather x1, waiting for transfers between devices, local(): lax.all_gather(up_weight, 'shard', axis=0, tiled=True)  57.5 us
    all_gather x1, waiting for transfers between devices, local(): lax.all_gather(down_weight, 'shard', axis=0, tiled=True)  54.9 us
    reduce_scatter x1, waiting for transfers between devices, local(): lax.psum_scatter(column_term(first_in, qkv_grad).astype(jnp.bfloat16), 's...  53.6 us
    psum x1, blocking collectives, local(): lax.psum(gain1_own.astype(jnp.bfloat16), 'replica').astype(jnp.float32)  23.3 us
    dot_general x4, matrix products, left_product(): lax.dot_general(left, right, (((0,), (0,)), ((), ())), preferred_element_...  21.3 us
  transfers between devices with their start and end apart: 9, of which 8 were waited for; matrix products, arithmetic and copies ran while one was open for 11% of the time, Pallas kernels for 0%

commit v1 on v0

--- a/solution.py
+++ b/solution.py
@@ -9,6 +9,26 @@
 EPSILON = 1e-05
 TANH_SCALE = math.sqrt(2.0 / math.pi)
 CUBIC = 0.044715
+
+
+def _move_loads(m, row_dim):
+    m = jnp.moveaxis(m, 0, row_dim)
+    tile_out = m.shape
+    return m.reshape(
+        *tile_out[:row_dim], tile_out[row_dim] * tile_out[row_dim + 1], *tile_out[row_dim + 2 :]
+    )
+
+
+def register_stacks_all_here(shard_in, axis_key):
+    cores_n = lax.axis_size(axis_key)
+    outer = shard_in[None]
+    for ix in range(cores_n.bit_length() - 1):
+        m_next = 1 << ix
+        lower = lax.ppermute(outer, axis_key, tuple(((it, it ^ m_next) for it in range(cores_n))))
+        vec_out = jnp.stack([outer, lower], axis=0)
+        clean = lax.axis_index(axis_key) >> ix & 1
+        outer = jnp.where(clean == 0, vec_out, vec_out[::-1]).reshape(-1, *shard_in.shape)
+    return outer
 
 
 def product(left, right):
@@ -137,6 +157,10 @@
     down_weight,
     down_bias,
 ):
+
+    def choose_pools_in(raw, vals, which_dim):
+        return _move_loads(register_stacks_all_here(raw, vals), which_dim)
+
     (
         gain_one,
         bias_one,
@@ -161,7 +185,7 @@
         lax.all_gather(out_bias, "shard", axis=0, tiled=True),
         lax.all_gather(norm2_gain, "shard", axis=0, tiled=True),
         lax.all_gather(norm2_bias, "shard", axis=0, tiled=True),
-        lax.all_gather(up_weight, "shard", axis=0, tiled=True),
+        choose_pools_in(up_weight, "shard", which_dim=0),
         lax.all_gather(up_bias, "shard", axis=0, tiled=True),
         lax.all_gather(down_weight, "shard", axis=0, tiled=True),
         lax.all_gather(down_bias, "shard", axis=0, tiled=True),

time: 688 us -> 740 us (1.076)
  blocking collectives: 82.4 us -> 231 us
  waiting for transfers between devices: 493 us -> 360 us
  other arithmetic: 22.1 us -> 50.2 us
    all_gather x1, blocking collectives: 6.02 us -> 155 us  [local(): lax.all_gather(out_bias, 'shard', axis=0, tiled=True)]
    all_gather x1 -> x0, waiting for transfers between devices: 57.5 us -> none  [local(): lax.all_gather(up_weight, 'shard', axis=0, tiled=True)]
    all_gather x1, waiting for transfers between devices: 54.9 us -> 0.02 us  [local(): lax.all_gather(down_weight, 'shard', axis=0, tiled=True)]
    all_gather x1, waiting for transfers between devices: 18.7 us -> 0.02 us  [local(): lax.all_gather(out_weight, 'shard', axis=0, tiled=True)]
    another operation x0 -> x3, other arithmetic: none -> 14.6 us  [register_stacks_all_here(): vec_out = jnp.stack([outer, lower], axis=0)]
    select_n x0 -> x1, other arithmetic: none -> 13.5 us  [register_stacks_all_here(): jnp.where(clean == 0, vec_out, vec_out[::-1]).reshape(-1, *shard_in.shape)]
  transfers between devices with their start and end apart: 9 -> 10, of which waited for: 8 -> 5; matrix products, arithmetic and copies ran while one was open for 11% -> 14% of each run, Pallas kernels for 0% -> 0%
where the time goes in v1:
time: 740 us; the launch traced here: 739 us
  waiting for transfers between devices  360 us (49%)
  blocking collectives  231 us (31%)
  matrix products  73.7 us (10%)
  other arithmetic  50.2 us (7%)
  between operations  15.9 us (2%)
    all_gather x1, blocking collectives, local(): lax.all_gather(out_bias, 'shard', axis=0, tiled=True)  155 us
    psum x1, waiting for transfers between devices, local(): lax.psum(qkv_owned, 'replica').astype(jnp.float32)  152 us
    reduce_scatter x1, waiting for transfers between devices, local(): lax.psum_scatter(column_term(second_in, pre_round).astype(jnp.bfloat16),...  74 us
    reduce_scatter x1, waiting for transfers between devices, local(): lax.psum_scatter(column_term(activated, out_grad).astype(jnp.bfloat16), '...  73.9 us
    reduce_scatter x1, waiting for transfers between devices, local(): lax.psum_scatter(column_term(first_in, qkv_grad).astype(jnp.bfloat16), 's...  53.7 us
    psum x1, blocking collectives, local(): lax.psum(gain1_own.astype(jnp.bfloat16), 'replica').astype(jnp.float32)  23 us
    dot_general x4, matrix products, right_product(): lax.dot_general(left, right, (((1,), (1,)), ((), ())), preferred_element_...  22.3 us
    dot_general x4, matrix products, left_product(): lax.dot_general(left, right, (((0,), (0,)), ((), ())), preferred_element_...  21.3 us
  transfers between devices with their start and end apart: 10, of which 5 were waited for; matrix products, arithmetic and copies ran while one was open for 14% of the time, Pallas kernels for 0%

profile of v1, /device:TPU:0, one launch (start us, length us, event | category | flops | bytes accessed | tf_op | source)
XLA Modules:
  0.0 739.1 jit_solution(15148538930673795989)
XLA Ops:
  7.2 0.7 all-gather.12.cloned.1.call-update
  8.0 0.7 all-gather.14.cloned.1.call-update
  8.7 0.7 all-gather.16.cloned.1.call-update
  9.5 0.6 collective-permute-start
  10.0 3.9 collective-permute-done
  13.9 2.0 pad_maximum_fusion.1
  16.0 5.1 fusion.3
  21.2 3.1 collective-permute-start.1
  24.3 154.9 %all-gather.4 = bf16[4,1,256]{2,1,0:T(2,128)(2,1)S(1)} all-gather(bf16[1,1,256]{2,1,0:T(2,128)(2,1)S(1)} %reshape.295), channel_id=1, replica_groups=mesh['replica'=8,'shard'=4] {'shard'}, dimensions={0}, use_global_device_ids=true | all-gather | bytes 2560 | tf_op jit(solution)/shard_map/all_gather | solution.py:185
  179.2 5.2 all-gather.1
  184.5 5.2 all-gather
  189.7 5.2 all-gather.3
  194.9 5.2 all-gather.2
  200.3 5.2 all_gather.45
  205.5 5.1 all-gather.6
  210.6 5.2 all-gather.5
  216.4 7.5 %pad_maximum_fusion = bf16[2,2,256,4096]{3,2,1,0:T(8,128)(2,1)} fusion(bf16[1,2,256,4096]{3,2,1,0:T(8,128)(2,1)} %bitcast.19, bf16[1,2,256,4096]{3,2,1,0:T(8,128)(2,1)} %get-tuple-element.47), kind=kLoop, calls=%fused_computation.3 | loop fusion | flops 4194304 | bytes 16777216 | tf_op jit(solution)/shard_map/stack | solution.py:28
  223.8 13.5 %reverse_select_fusion = bf16[2,2,256,4096]{3,2,1,0:T(8,128)(2,1)} fusion(bf16[2,2,256,4096]{3,2,1,0:T(8,128)(2,1)} %pad_maximum_fusion, pred[]{:T(512)S(6)} %eq.28), kind=kLoop, calls=%fused_computation.2 | loop fusion | flops 4194304 | bytes 16777216 | tf_op jit(solution)/shard_map/jit(_where)/select_n | solution.py:30
  237.4 3.9 fusion.68
  241.9 0.4 convolution_multiply_fusion.1
  242.3 0.5 convolution_convert_fusion.6
  242.8 2.2 fusion.73
  245.3 4.8 convolution_add_fusion
  250.1 6.9 fusion.76
  257.1 7.0 multiply_reduce_fusion.1
  264.1 0.3 fusion.70
  264.4 2.0 convolution_convert_fusion.3
  266.5 3.0 fusion.15
  269.5 1.5 convolution_convert_fusion.5
  271.0 1.8 copy.63
  272.8 3.2 fusion.71
  276.0 2.4 fusion.77
  278.4 3.6 convolution_convert_fusion.4
  281.9 3.7 fusion.72
  285.7 5.8 convolution_convert_fusion.2
  291.5 6.6 convolution_convert_fusion
  298.1 0.3 reduce-scatter.9.cloned.1.call-start
  298.4 6.9 convolution_convert_fusion.1
  305.4 53.7 %reduce-scatter.5.cloned.1.call-done = bf16[256,3072]{1,0:T(8,128)(2,1)} async-done(((bf16[1024,3072]{1,0:T(8,128)(2,1)}), bf16[256,3072]{1,0:T(8,128)(2,1)}) %reduce-scatter.5.cloned.1.call-update) | async-done | bytes 1572880 | tf_op jit(solution)/shard_map/reduce_scatter | solution.py:255
  359.1 73.9 %reduce-scatter.11.cloned.1.call-done = bf16[1024,1024]{1,0:T(8,128)(2,1)} async-done(((bf16[4096,1024]{1,0:T(8,128)(2,1)}), bf16[1024,1024]{1,0:T(8,128)(2,1)}) %reduce-scatter.11.cloned.1.call-update) | async-done | bytes 2097168 | tf_op jit(solution)/shard_map/reduce_scatter | solution.py:221
  432.9 74.0 %reduce-scatter.9.cloned.1.call-done = bf16[256,4096]{1,0:T(8,128)(2,1)} async-done(((bf16[1024,4096]{1,0:T(8,128)(2,1)}), bf16[256,4096]{1,0:T(8,128)(2,1)}) %reduce-scatter.9.cloned.1.call-update) | async-done | bytes 2097168 | tf_op jit(solution)/shard_map/reduce_scatter | solution.py:231
  507.0 0.6 copy-done.24
  507.6 5.1 all-gather.7
  512.7 1.0 reduce_sum.202
  513.7 0.6 dynamic-slice
  515.7 6.8 fusion.39
  522.6 11.3 %all-reduce.11 = (bf16[1024]{0:T(1024)(128)(2,1)S(1)}, bf16[1024]{0:T(1024)(128)(2,1)S(1)}, bf16[1024]{0:T(1024)(128)(2,1)S(1)}, bf16[1024]{0:T(1024)(128)(2,1)S...) all-reduce(bf16[1024]{0:T(1024)(128)(2,1)S(1)} %get-tuple-element.1, ...), channel_id=2, replica_groups=mesh['replica'=8,'shard'=4] {'shard'}, use_global_device_ids=true, to_apply=%region_13.14.clone | all-reduce | flops 12288 | bytes 49152
  534.5 23.0 %all-reduce.9 = (bf16[256]{0:T(256)(128)(2,1)S(1)}, bf16[256]{0:T(256)(128)(2,1)S(1)}, bf16[256]{0:T(256)(128)(2,1)S(1)}, bf16[256]{0:T(256)(128)(2,1)S(1)}, bf1...) all-reduce(bf16[256]{0:T(256)(128)(2,1)S(1)} %dynamic-slice.1, ...), channel_id=1, replica_groups=mesh['replica'=8,'shard'=4] {'replica'}, use_global_device_ids=true, to_apply=%region_14.15 | all-reduce | flops 3072 | bytes 12288 | tf_op jit(solution)/shard_map/psum | solution.py:318
  557.5 0.6 convert_element_type.228
  558.0 0.6 convert_element_type.230
  558.6 0.6 convert_element_type.235
  559.2 0.6 convert_element_type.238
  559.7 0.6 convert_element_type.242
  560.3 0.6 convert_element_type.244
  560.9 0.6 convert_element_type.246
  561.4 0.6 convert_element_type.250
  562.0 0.6 convert_element_type.253
  562.6 2.0 fusion.38
  564.6 5.6 fusion.19
  570.2 152.3 %all-reduce.14.cloned.1.call-done = (bf16[256,3072]{1,0:T(8,128)(2,1)}, bf16[256,1024]{1,0:T(8,128)(2,1)}, bf16[256,4096]{1,0:T(8,128)(2,1)}, bf16[1024,1024]{1,0:T(8,128)(2,1)}) async-done(((bf16[256,3072]{1,0:T(8,128)(2,1)}, bf16[256,1024]{1,0:T(8,128)(2,1)}, bf16[256,4096]{1,0:T(8,128)(2,1)}, bf16[1024,1024]{1,0:T(8,128)(2,1)}), (bf16[256,3072]{1,0:T(8,128)(2,1)}, bf16[256,1024]{1,0:T(8,128)(2,1)}, ...) | async-done | bytes 6291472 | tf_op jit(solution)/shard_map/psum | solution.py:320
  722.6 3.6 convert_element_type.232
  726.2 1.1 convert_element_type.240
  727.3 2.5 convert_element_type.248
  729.8 2.5 convert_element_type.252
  (114 shorter events, 3.0 us)
Async XLA Ops:
  7.2 2.3 copy-start.7
  7.2 230.2 %all-gather.12.cloned.1.call-start = ((), (), s32[]{:S(2)}) async-start(), calls=%async_computation.4 | async-start | bytes 7864320 | tf_op jit(solution)/shard_map/all_gather | solution.py:181
  7.9 234.9 %all-gather.14.cloned.1.call-start = ((), (), s32[]{:S(2)}) async-start(), calls=%async_computation.5 | async-start | bytes 2621440 | tf_op jit(solution)/shard_map/all_gather | solution.py:184
  8.7 241.4 %all-gather.16.cloned.1.call-start = ((), (), s32[]{:S(2)}) async-start(), calls=%async_computation.6 | async-start | bytes 10485760 | tf_op jit(solution)/shard_map/all_gather | solution.py:190
  9.4 296.0 %reduce-scatter.7.cloned.1.call-start = ((), (), s32[]{:S(2)}) async-start(), calls=%async_computation.8 | async-start | bytes 2621440 | tf_op jit(solution)/shard_map/reduce_scatter | solution.py:242
  9.5 4.5 collective-permute-start
  15.9 8.4 %copy-start.16 = (bf16[256]{0:T(256)(128)(2,1)S(1)}, bf16[256]{0:T(256)(128)(2,1)}, u32[]{:S(2)}) copy-start(bf16[256]{0:T(256)(128)(2,1)} %param.25) | copy-start | bytes 1540
  15.9 163.3 %copy-start.17 = (bf16[256]{0:T(256)(128)(2,1)S(1)}, bf16[256]{0:T(256)(128)(2,1)}, u32[]{:S(2)}) copy-start(bf16[256]{0:T(256)(128)(2,1)} %param.20) | copy-start | bytes 1540
  15.9 168.5 %copy-start.18 = (bf16[256]{0:T(256)(128)(2,1)S(1)}, bf16[256]{0:T(256)(128)(2,1)}, u32[]{:S(2)}) copy-start(bf16[256]{0:T(256)(128)(2,1)} %param.19) | copy-start | bytes 1540
  16.0 173.7 %copy-start.19 = (bf16[256]{0:T(256)(128)(2,1)S(1)}, bf16[256]{0:T(256)(128)(2,1)}, u32[]{:S(2)}) copy-start(bf16[256]{0:T(256)(128)(2,1)} %param.22) | copy-start | bytes 1540
  16.0 178.9 %copy-start.20 = (bf16[256]{0:T(256)(128)(2,1)S(1)}, bf16[256]{0:T(256)(128)(2,1)}, u32[]{:S(2)}) copy-start(bf16[256]{0:T(256)(128)(2,1)} %param.23) | copy-start | bytes 1540
  16.0 184.2 %copy-start.21 = (s32[1,4]{1,0:T(1,128)S(1)}, s32[1,4]{1,0:T(1,128)}, u32[]{:S(2)}) copy-start(s32[1,4]{1,0:T(1,128)} %param.18) | copy-start | bytes 52
  16.0 184.3 %copy-start.15 = (bf16[1024]{0:T(1024)(128)(2,1)S(1)}, bf16[1024]{0:T(1024)(128)(2,1)}, u32[]{:S(2)}) copy-start(bf16[1024]{0:T(1024)(128)(2,1)} %param.29) | copy-start | bytes 6148
  16.0 189.5 %copy-start.22 = (bf16[256]{0:T(256)(128)(2,1)S(1)}, bf16[256]{0:T(256)(128)(2,1)}, u32[]{:S(2)}) copy-start(bf16[256]{0:T(256)(128)(2,1)} %param.27) | copy-start | bytes 1540
  16.0 194.6 %copy-start.23 = (bf16[256]{0:T(256)(128)(2,1)S(1)}, bf16[256]{0:T(256)(128)(2,1)}, u32[]{:S(2)}) copy-start(bf16[256]{0:T(256)(128)(2,1)} %param.26) | copy-start | bytes 1540
  16.0 199.9 %copy-start = (bf16[128,1024]{1,0:T(8,128)(2,1)S(1)}, bf16[128,1024]{1,0:T(8,128)(2,1)}, u32[]{:S(2)}) copy-start(bf16[128,1024]{1,0:T(8,128)(2,1)} %param.16) | copy-start | bytes 786436
  21.2 195.2 %collective-permute-start.1 = (bf16[2,256,4096]{2,1,0:T(8,128)(2,1)}, bf16[2,256,4096]{2,1,0:T(8,128)(2,1)}, u32[]{:S(2)}, u32[]{:S(2)}) collective-permute-start(bf16[2,256,4096]{2,1,0:T(8,128)(2,1)} %get-tuple-element.48), channel_id=1, source_target_pairs={{0,2},{1,3},{2,0},{3,1},{4,6},{5,7},{6,4},{7,5},{8,10},{9,11},{10,... | collective-permute-start | bytes 12582920 | tf_op jit(solution)/shard_map/ppermute | solution.py:27
  241.6 1.2 copy-start.10
  241.7 3.3 copy-start.11
  241.9 0.9 copy-start.9
  242.3 2.8 copy-start.8
  242.8 2.5 copy-start.12
  245.3 4.8 copy-start.3
  257.0 7.1 copy-start.2
  257.0 7.1 copy-start.4
  257.1 7.3 copy-start.13
  266.4 92.6 %reduce-scatter.5.cloned.1.call-start = ((), (), s32[]{:S(2)}) async-start(), calls=%async_computation.7 | async-start | bytes 7864320 | tf_op jit(solution)/shard_map/reduce_scatter | solution.py:255
  266.5 3.0 copy-start.1
  291.5 141.5 %reduce-scatter.11.cloned.1.call-start = ((), (), s32[]{:S(2)}) async-start(), calls=%async_computation.10 | async-start | bytes 10485760 | tf_op jit(solution)/shard_map/reduce_scatter | solution.py:221
  298.1 208.8 %reduce-scatter.9.cloned.1.call-start = ((), (), s32[]{:S(2)}) async-start(), calls=%async_computation.9 | async-start | bytes 10485760 | tf_op jit(solution)/shard_map/reduce_scatter | solution.py:231
  305.3 417.2 %all-reduce.14.cloned.1.call-start = ((), (), s32[]{:S(2)}) async-start(), calls=%async_computation.11 | async-start | bytes 12582912 | tf_op jit(solution)/shard_map/psum | solution.py:320
  506.9 0.7 copy-start.24
  506.9 6.7 copy-start.25
  722.6 3.6 copy-start.14
  722.6 4.7 copy-start.6
  727.3 2.5 copy-start.5
Sparse Core Ops, SparseCore 0:
  9.6 80.5 all-gather.11
  91.7 33.0 all-gather.13
  126.4 78.4 all-gather.15
  266.5 31.2 reduce-scatter.6
  300.2 58.8 reduce-scatter.4
  361.5 71.3 reduce-scatter.10
  435.5 71.3 reduce-scatter.8
  511.4 211.1 all-reduce.13
